TPU v7x, 128 devices: a whole 4x4x4 slice. The times are simulated.
128 devices in a mesh: row: 8 (over z_hi, y), col: 16 (over x, z_lo, core).
Axes of the slice: x: 4, y: 4, z: 4 (z_hi: 2, z_lo: 2; z = z_hi * 2 + z_lo), core: 2. Of those that a mesh axis runs over, the one named last changes fastest.
Arguments:
- features: bfloat16 [16, 8192, 128], P('col', 'row'), may hold values from 0.099609375 to 3
- relu_mask: int32 [16, 8192, 128], P('col', 'row'), may hold values 0 or 1
- tiles: bfloat16 [8, 16, 184, 256, 256], P('row', 'col'), may hold values from -0.25 to 0.25
- tile_rows: int32 [8, 16, 184], P('row', 'col'), may hold values from 0 to 63, as said below
- tile_cols: int32 [8, 16, 184], P('row', 'col'), may hold values from 0 to 31
- tile_count: int32 [8, 16], P('row', 'col'), may hold values from 23 to 184, as said below
- weight: bfloat16 [128, 128], replicated, may hold values from -0.5 to 0.5
- cotangent: bfloat16 [8, 16384, 128], P('row', 'col'), may hold values from -6 to 6
Outputs:
- out_pre: bfloat16 [8, 16384, 128], P('row', 'col')
- weight_grad: float32 [128, 128], replicated
- input_grad: bfloat16 [16, 8192, 128], P('col', 'row')
Inputs may be any that keep to these rules, and one draw needn't show every extreme that they name: `tile_rows`: within one panel pair the live and dead slots name distinct (block row, block column) pairs. `tile_count`: counts differ widely between panel pairs.
All inputs are finite; a program needn't handle non-finite values. No bound on the sum of `relu_mask` on one device may be relied on, other than what follows from the above.
Results may differ from a plain program's by a relative error of at most 0.022.
Values may be sent and summed in bfloat16 or wider, within the bound.
A program may use at most 192 MiB of HBM per device.

v0:
```python
import jax
import jax.numpy as jnp
from jax import lax
from jax.sharding import PartitionSpec as P


def slot_products(tile_vals, row_ids, col_ids, source, backward):
    tile_size = tile_vals.shape[1]
    feature_width = source.shape[1]
    if backward:
        blocks = source.reshape(-1, tile_size, feature_width)[row_ids]
        products = jnp.einsum("sij,sif->sjf", tile_vals, blocks, preferred_element_type=jnp.float32)
        target_ids = col_ids
    else:
        blocks = source.reshape(-1, tile_size, feature_width)[col_ids]
        products = jnp.einsum("sij,sjf->sif", tile_vals, blocks, preferred_element_type=jnp.float32)
        target_ids = row_ids
    return (products, target_ids)


def apply_tiles(tile_vals, row_ids, col_ids, live_count, source, backward, segments):
    feature_width = source.shape[1]
    slots = tile_vals.shape[0]
    products, target_ids = slot_products(tile_vals, row_ids, col_ids, source, backward)
    live_slots = jnp.arange(slots, dtype=jnp.int32) < live_count
    targets = jnp.arange(segments, dtype=jnp.int32)[:, None] == target_ids[None, :]
    selector = jnp.where(targets & live_slots[None, :], 1.0, 0.0).astype(jnp.float32)
    total = jnp.einsum(
        "rs,sif->rif",
        selector,
        products,
        precision=lax.Precision.HIGHEST,
        preferred_element_type=jnp.float32,
    )
    return total.reshape(-1, feature_width)


def body(features, relu_mask, tiles, tile_rows, tile_cols, tile_count, weight, cotangent):
    tile_size = tiles.shape[3]
    mask_rows = relu_mask[0]
    hidden = features[0] * mask_rows.astype(jnp.bfloat16)
    tile_vals = tiles[0, 0]
    row_ids = tile_rows[0, 0]
    col_ids = tile_cols[0, 0]
    live_count = tile_count[0, 0]
    own_rows = hidden.shape[0]
    row_blocks = own_rows * lax.axis_size("col") // tile_size
    col_blocks = own_rows * lax.axis_size("row") // tile_size
    feat_panel = lax.all_gather(hidden, "row", axis=0, tiled=True)
    forward_terms = apply_tiles(
        tile_vals, row_ids, col_ids, live_count, feat_panel, False, row_blocks
    )
    forward_terms = lax.optimization_barrier(forward_terms.astype(jnp.bfloat16)).astype(jnp.float32)
    aggregate = lax.psum_scatter(
        forward_terms.astype(jnp.bfloat16), "col", scatter_dimension=0, tiled=True
    )
    out_pre = jnp.dot(aggregate, weight, preferred_element_type=jnp.float32).astype(jnp.bfloat16)
    cot_rows = cotangent[0]
    weight_term = lax.dot_general(
        aggregate, cot_rows, (((0,), (0,)), ((), ())), preferred_element_type=jnp.float32
    )
    grad_scale = 1.0 / jnp.sqrt(jnp.float32(own_rows * lax.axis_size("row") * lax.axis_size("col")))
    weight_grad = lax.psum(weight_term, ("row", "col")) * grad_scale
    grad_rows = lax.dot_general(
        cot_rows, weight, (((1,), (1,)), ((), ())), preferred_element_type=jnp.float32
    )
    grad_rows = lax.all_gather(grad_rows.astype(jnp.bfloat16), "col", axis=0, tiled=True)
    back_terms = apply_tiles(tile_vals, row_ids, col_ids, live_count, grad_rows, True, col_blocks)
    back_terms = lax.optimization_barrier(back_terms.astype(jnp.bfloat16)).astype(jnp.float32)
    summed = lax.psum_scatter(
        back_terms.astype(jnp.bfloat16), "row", scatter_dimension=0, tiled=True
    ).astype(jnp.float32)
    input_grad = (summed * mask_rows.astype(jnp.float32)).astype(jnp.bfloat16)
    return (out_pre[None], weight_grad, input_grad[None])


def solution(mesh):
    placed = (
        P("col", "row", None),
        P("col", "row", None),
        P("row", "col", None, None, None),
        P("row", "col", None),
        P("row", "col", None),
        P("row", "col"),
        P(),
        P("row", "col", None),
    )
    return jax.shard_map(
        body,
        mesh=mesh,
        in_specs=placed,
        out_specs=(P("row", "col", None), P(), P("col", "row", None)),
        check_vma=False,
    )
```

profile of v0, /device:TPU:1, one launch (start us, length us, event | category | flops | bytes accessed | tf_op | source)
XLA Modules:
  0.0 451.2 jit_solution(6644754055595961643)
XLA Ops:
  7.2 0.0 copy-start
  7.2 0.0 all-gather.6.cloned.1.call-start
  7.2 1.9 convert_multiply_fusion
  9.1 0.0 all-gather.6.cloned.1.call-update
  9.1 0.0 all-gather.4.cloned.1.call-start
  9.2 0.0 copy-done
  9.2 1.7 convolution_convert_fusion
  10.9 0.0 all-gather.4.cloned.1.call-update
  10.9 0.0 reduce-scatter.3.cloned.1.call-start
  11.6 0.7 compare_select_fusion.1
  12.3 55.5 %all-gather.6.cloned.1.call-done = bf16[1,8192,128]{2,1,0:T(8,128)(2,1)} async-done(((bf16[1,1024,128]{2,1,0:T(8,128)(2,1)}), bf16[1,8192,128]{2,1,0:T(8,128)(2,1)}) %all-gather.6.cloned.1.call-update) | async-done | bytes 2097168 | tf_op jit(solution)/shard_map/all_gather | solution.py:49
  67.9 9.7 %gather_fusion = bf16[184,256,128]{2,1,0:T(8,128)(2,1)} fusion(bf16[32,256,128]{2,1,0:T(8,128)(2,1)} %bitcast.56, s32[1024]{0:T(1024)S(1)} %pad_clamp_fusion.1), kind=kCustom, calls=%fused_computation | custom fusion | bytes 24117984 | tf_op jit(solution)/shard_map/gather | solution.py:15
  77.5 21.6 %fusion.6 = f32[184,128,256]{2,1,0:T(8,128)} fusion(bf16[184,256,128]{2,1,0:T(8,128)(2,1)} %gather_fusion, bf16[1,1,184,256,256]{4,3,2,1,0:T(8,128)(2,1)} %param.10), kind=kOutput, calls=%fused_computation.8 | convolution fusion | flops 3087007744 | bytes 60293120 | tf_op jit(solution)/shard_map/sij,sjf->sif/dot_general | solution.py:16
  99.1 0.0 copy-start.3
  99.1 24.6 %copy.13 = f32[184,128,256]{1,0,2:T(8,128)} copy(f32[184,128,256]{2,1,0:T(8,128)} %fusion.6) | data formatting | bytes 48234496 | tf_op jit(solution)/shard_map/sij,sjf->sif/dot_general | solution.py:16
  123.7 0.0 copy-done.3
  123.7 20.8 %fusion.8 = bf16[64,256,128]{2,0,1:T(8,128)(2,1)S(1)} fusion(f32[184,128,256]{1,0,2:T(8,128)} %copy.13, s32[184]{0:T(256)S(1)} %bitcast.60, pred[184]{0:T(512)(128)(4,1)S(1)} %iota_compare_fusion.2), kind=kOutput, calls=%fused_computation.10 | convolution fusion | flops 4632644096 | bytes 28312472 | tf_op jit(solution)/shard_map/rs,sif->rif/dot_general | solution.py:28
  144.5 4.7 %copy.11 = bf16[64,256,128]{2,1,0:T(8,128)(2,1)} copy(bf16[64,256,128]{2,0,1:T(8,128)(2,1)S(1)} %fusion.8) | data formatting | bytes 8388608 | tf_op jit(solution)/shard_map/convert_element_type | solution.py:53
  149.1 0.0 reduce-scatter.3.cloned.1.call-update
  149.2 0.0 reduce-scatter.5.cloned.1.call-start
  149.2 0.0 all-gather.4.cloned.1.call-done
  149.3 10.3 %gather_fusion.1 = bf16[184,256,128]{2,1,0:T(8,128)(2,1)} fusion(bf16[64,256,128]{2,1,0:T(8,128)(2,1)} %bitcast.57, s32[1024]{0:T(1024)S(1)} %pad_clamp_fusion), kind=kCustom, calls=%fused_computation.1 | custom fusion | bytes 24117984 | tf_op jit(solution)/shard_map/gather | solution.py:11
  159.5 22.0 %fusion.4 = f32[184,128,256]{2,1,0:T(8,128)} fusion(bf16[184,256,128]{2,1,0:T(8,128)(2,1)} %gather_fusion.1, bf16[1,1,184,256,256]{4,3,2,1,0:T(8,128)(2,1)} %param.10), kind=kOutput, calls=%fused_computation.6 | convolution fusion | flops 3087007744 | bytes 60293120 | tf_op jit(solution)/shard_map/sij,sif->sjf/dot_general | solution.py:12
  181.6 0.0 copy-start.4
  181.6 24.6 %copy.14 = f32[184,128,256]{1,0,2:T(8,128)} copy(f32[184,128,256]{2,1,0:T(8,128)} %fusion.4) | data formatting | bytes 48234496 | tf_op jit(solution)/shard_map/sij,sif->sjf/dot_general | solution.py:12
  206.2 0.0 copy-done.4
  206.2 0.0 copy-start.2
  206.2 0.0 copy-start.1
  206.2 17.1 %fusion.11 = bf16[32,256,128]{2,0,1:T(8,128)(2,1)S(1)} fusion(f32[184,128,256]{1,0,2:T(8,128)} %copy.14, s32[184]{0:T(256)S(1)} %bitcast.61, pred[184]{0:T(512)(128)(4,1)S(1)} %iota_compare_fusion.2), kind=kOutput, calls=%fused_computation.11 | convolution fusion | flops 2316322048 | bytes 26215320 | tf_op jit(solution)/shard_map/rs,sif->rif/dot_general | solution.py:28
  223.3 2.1 copy.12
  225.4 0.0 reduce-scatter.5.cloned.1.call-update
  225.4 0.0 all-reduce.2.cloned.1.call-start
  225.5 0.0 reduce-scatter.3.cloned.1.call-done
  225.5 1.9 fusion.18
  227.4 0.0 all-reduce.2.cloned.1.call-update
  227.4 0.0 copy-done.2
  227.4 1.9 fusion.14
  229.3 70.3 %reduce-scatter.5.cloned.1.call-done = bf16[1024,128]{1,0:T(8,128)(2,1)} async-done(((bf16[8192,128]{1,0:T(8,128)(2,1)}), bf16[1024,128]{1,0:T(8,128)(2,1)}) %reduce-scatter.5.cloned.1.call-update) | async-done | bytes 262160 | tf_op jit(solution)/shard_map/reduce_scatter | solution.py:70
  299.6 0.0 copy-done.1
  299.6 1.7 fusion.16
  301.3 141.9 %all-reduce.2.cloned.1.call-done = f32[128,128]{1,0:T(8,128)} async-done(((f32[128,128]{1,0:T(8,128)}), f32[128,128]{1,0:T(8,128)}) %all-reduce.2.cloned.1.call-update) | async-done | bytes 65552 | tf_op jit(solution)/shard_map/psum | solution.py:63
  443.2 1.5 broadcast_multiply_fusion
  (4 shorter events, 0.0 us)
Async XLA Ops:
  7.2 2.0 copy-start
  7.2 60.7 %all-gather.6.cloned.1.call-start = ((), (), s32[]{:S(2)}) async-start(), calls=%async_computation.6 | async-start | bytes 2359296 | tf_op jit(solution)/shard_map/all_gather | solution.py:49
  9.1 140.1 %all-gather.4.cloned.1.call-start = ((), (), s32[]{:S(2)}) async-start(), calls=%async_computation.4 | async-start | bytes 4456448 | tf_op jit(solution)/shard_map/all_gather | solution.py:67
  10.9 214.6 %reduce-scatter.3.cloned.1.call-start = ((), (), s32[]{:S(2)}) async-start(), calls=%async_computation.2 | async-start | bytes 4456448 | tf_op jit(solution)/shard_map/reduce_scatter | solution.py:54
  99.1 24.6 %copy-start.3 = (s32[1,1,184]{2,1,0:T(1,128)S(1)}, s32[1,1,184]{2,1,0:T(1,128)}, u32[]{:S(2)}) copy-start(s32[1,1,184]{2,1,0:T(1,128)} %param.11) | copy-start | bytes 2212
  149.2 150.4 %reduce-scatter.5.cloned.1.call-start = ((), (), s32[]{:S(2)}) async-start(), calls=%async_computation.5 | async-start | bytes 2359296 | tf_op jit(solution)/shard_map/reduce_scatter | solution.py:70
  181.6 24.6 %copy-start.4 = (s32[1,1,184]{2,1,0:T(1,128)S(1)}, s32[1,1,184]{2,1,0:T(1,128)}, u32[]{:S(2)}) copy-start(s32[1,1,184]{2,1,0:T(1,128)} %param.12) | copy-start | bytes 2212
  206.2 21.2 %copy-start.2 = (bf16[128,128]{1,0:T(8,128)(2,1)S(1)}, bf16[128,128]{1,0:T(8,128)(2,1)}, u32[]{:S(2)}) copy-start(bf16[128,128]{1,0:T(8,128)(2,1)} %param.14) | copy-start | bytes 98308
  206.2 93.4 %copy-start.1 = (s32[1,1024,128]{2,1,0:T(8,128)S(1)}, s32[1,1024,128]{2,1,0:T(8,128)}, u32[]{:S(2)}) copy-start(s32[1,1024,128]{2,1,0:T(8,128)} %param.9) | copy-start | bytes 1572868
  225.4 217.8 %all-reduce.2.cloned.1.call-start = ((), (), s32[]{:S(2)}) async-start(), calls=%async_computation.3 | async-start | bytes 131072 | tf_op jit(solution)/shard_map/psum | solution.py:63
Sparse Core Ops, SparseCore 0:
  10.9 56.9 all-gather.5
  70.1 37.8 all-gather.3
  149.3 63.9 reduce-scatter.2
  225.6 74.0 reduce-scatter.4
  305.5 137.6 all-reduce.1
where the time goes:
time: 452 us; the launch traced here: 451 us
  waiting for transfers between devices  268 us (59%)
  matrix products  86.9 us (19%)
  local copies, waits for them, and re-layouts  75.9 us (17%)
  between operations  14.5 us (3%)
  other arithmetic  5.8 us (1%)
    psum x1, waiting for transfers between devices, body(): weight_grad = lax.psum(weight_term, ('row', 'col')) * grad_scale  142 us
    reduce_scatter x1, waiting for transfers between devices, body(): lax.psum_scatter(back_terms.astype(jnp.bfloat16), 'row', scatter_dimensio...  70.3 us
    all_gather x1, waiting for transfers between devices, body(): feat_panel = lax.all_gather(hidden, 'row', axis=0, tiled=True)  55.5 us
    dot_general x2, matrix products, apply_tiles(): jnp.einsum('rs,sif->rif', selector, products, precision=lax.Precision.HIG...  37.8 us
    dot_general x1, local copies, waits for them, and re-layouts, slot_products(): jnp.einsum('sij,sif->sjf', tile_vals, blocks, preferred_element_type=jnp....  24.6 us
    dot_general x1, local copies, waits for them, and re-layouts, slot_products(): jnp.einsum('sij,sjf->sif', tile_vals, blocks, preferred_element_type=jnp....  24.6 us
    dot_general x1, matrix products, slot_products(): jnp.einsum('sij,sif->sjf', tile_vals, blocks, preferred_element_type=jnp....  22 us
    dot_general x1, matrix products, slot_products(): jnp.einsum('sij,sjf->sif', tile_vals, blocks, preferred_element_type=jnp....  21.6 us
  transfers between devices with their start and end apart: 5, of which 3 were waited for; matrix products, arithmetic and copies ran while one was open for 37% of the time, Pallas kernels for 0%

commit v1 on v0

--- a/solution.py
+++ b/solution.py
@@ -60,7 +60,7 @@
         aggregate, cot_rows, (((0,), (0,)), ((), ())), preferred_element_type=jnp.float32
     )
     grad_scale = 1.0 / jnp.sqrt(jnp.float32(own_rows * lax.axis_size("row") * lax.axis_size("col")))
-    weight_grad = lax.psum(weight_term, ("row", "col")) * grad_scale
+    weight_grad = jnp.sum(lax.all_gather(weight_term, ("row", "col")), axis=0) * grad_scale
     grad_rows = lax.dot_general(
         cot_rows, weight, (((1,), (1,)), ((), ())), preferred_element_type=jnp.float32
     )

time: 452 us -> 517 us (1.14)
  waiting for transfers between devices: 268 us -> 329 us
    all_gather x0 -> x1, waiting for transfers between devices: none -> 203 us  [body(): lax.all_gather(weight_term, ('row', 'col'))]
    psum x1 -> x0, waiting for transfers between devices: 142 us -> none  [body(): weight_grad = lax.psum(weight_term, ('row', 'col')) * grad_scale]
  transfers between devices with their start and end apart: 5 -> 5, of which waited for: 3 -> 3; matrix products, arithmetic and copies ran while one was open for 37% -> 32% of each run, Pallas kernels for 0% -> 0%
where the time goes in v1:
time: 517 us; the launch traced here: 516 us
  waiting for transfers between devices  329 us (64%)
  matrix products  86.9 us (17%)
  local copies, waits for them, and re-layouts  76 us (15%)
  between operations  14.5 us (3%)
  other arithmetic  8.77 us (2%)
    all_gather x1, waiting for transfers between devices, body(): lax.all_gather(weight_term, ('row', 'col'))  203 us
    reduce_scatter x1, waiting for transfers between devices, body(): lax.psum_scatter(back_terms.astype(jnp.bfloat16), 'row', scatter_dimensio...  70.3 us
    all_gather x1, waiting for transfers between devices, body(): feat_panel = lax.all_gather(hidden, 'row', axis=0, tiled=True)  55.5 us
    dot_general x2, matrix products, apply_tiles(): jnp.einsum('rs,sif->rif', selector, products, precision=lax.Precision.HIG...  37.8 us
    dot_general x1, local copies, waits for them, and re-layouts, slot_products(): jnp.einsum('sij,sif->sjf', tile_vals, blocks, preferred_element_type=jnp....  24.6 us
    dot_general x1, local copies, waits for them, and re-layouts, slot_products(): jnp.einsum('sij,sjf->sif', tile_vals, blocks, preferred_element_type=jnp....  24.6 us
    dot_general x1, matrix products, slot_products(): jnp.einsum('sij,sif->sjf', tile_vals, blocks, preferred_element_type=jnp....  22 us
    dot_general x1, matrix products, slot_products(): jnp.einsum('sij,sjf->sif', tile_vals, blocks, preferred_element_type=jnp....  21.6 us
  transfers between devices with their start and end apart: 5, of which 3 were waited for; matrix products, arithmetic and copies ran while one was open for 32% of the time, Pallas kernels for 0%

profile of v1, /device:TPU:1, one launch (start us, length us, event | category | flops | bytes accessed | tf_op | source)
XLA Modules:
  0.0 515.7 jit_solution(16565796133954381582)
XLA Ops:
  7.2 0.0 copy-start
  7.2 0.0 all-gather.8.cloned.1.call-start
  7.2 1.9 convert_multiply_fusion
  9.1 0.0 all-gather.8.cloned.1.call-update
  9.1 0.0 all-gather.6.cloned.1.call-start
  9.2 0.0 copy-done
  9.2 1.7 convolution_convert_fusion
  10.9 0.0 all-gather.6.cloned.1.call-update
  10.9 0.0 reduce-scatter.3.cloned.1.call-start
  11.6 0.7 compare_select_fusion.1
  12.3 55.5 %all-gather.8.cloned.1.call-done = bf16[1,8192,128]{2,1,0:T(8,128)(2,1)} async-done(((bf16[1,1024,128]{2,1,0:T(8,128)(2,1)}), bf16[1,8192,128]{2,1,0:T(8,128)(2,1)}) %all-gather.8.cloned.1.call-update) | async-done | bytes 2097168 | tf_op jit(solution)/shard_map/all_gather | solution.py:49
  67.9 9.7 %gather_fusion = bf16[184,256,128]{2,1,0:T(8,128)(2,1)} fusion(bf16[32,256,128]{2,1,0:T(8,128)(2,1)} %bitcast.57, s32[1024]{0:T(1024)S(1)} %pad_clamp_fusion.1), kind=kCustom, calls=%fused_computation | custom fusion | bytes 24117984 | tf_op jit(solution)/shard_map/gather | solution.py:15
  77.5 21.6 %fusion.6 = f32[184,128,256]{2,1,0:T(8,128)} fusion(bf16[184,256,128]{2,1,0:T(8,128)(2,1)} %gather_fusion, bf16[1,1,184,256,256]{4,3,2,1,0:T(8,128)(2,1)} %param.10), kind=kOutput, calls=%fused_computation.8 | convolution fusion | flops 3087007744 | bytes 60293120 | tf_op jit(solution)/shard_map/sij,sjf->sif/dot_general | solution.py:16
  99.1 0.0 copy-start.3
  99.1 24.6 %copy.13 = f32[184,128,256]{1,0,2:T(8,128)} copy(f32[184,128,256]{2,1,0:T(8,128)} %fusion.6) | data formatting | bytes 48234496 | tf_op jit(solution)/shard_map/sij,sjf->sif/dot_general | solution.py:16
  123.7 0.0 copy-done.3
  123.7 20.8 %fusion.8 = bf16[64,256,128]{2,0,1:T(8,128)(2,1)S(1)} fusion(f32[184,128,256]{1,0,2:T(8,128)} %copy.13, s32[184]{0:T(256)S(1)} %bitcast.62, pred[184]{0:T(512)(128)(4,1)S(1)} %iota_compare_fusion.2), kind=kOutput, calls=%fused_computation.10 | convolution fusion | flops 4632644096 | bytes 28312472 | tf_op jit(solution)/shard_map/rs,sif->rif/dot_general | solution.py:28
  144.5 4.7 copy.11
  149.1 0.0 reduce-scatter.3.cloned.1.call-update
  149.2 0.0 reduce-scatter.5.cloned.1.call-start
  149.2 0.0 all-gather.6.cloned.1.call-done
  149.3 10.3 %gather_fusion.1 = bf16[184,256,128]{2,1,0:T(8,128)(2,1)} fusion(bf16[64,256,128]{2,1,0:T(8,128)(2,1)} %bitcast.58, s32[1024]{0:T(1024)S(1)} %pad_clamp_fusion), kind=kCustom, calls=%fused_computation.1 | custom fusion | bytes 24117984 | tf_op jit(solution)/shard_map/gather | solution.py:11
  159.5 22.0 %fusion.4 = f32[184,128,256]{2,1,0:T(8,128)} fusion(bf16[184,256,128]{2,1,0:T(8,128)(2,1)} %gather_fusion.1, bf16[1,1,184,256,256]{4,3,2,1,0:T(8,128)(2,1)} %param.10), kind=kOutput, calls=%fused_computation.6 | convolution fusion | flops 3087007744 | bytes 60293120 | tf_op jit(solution)/shard_map/sij,sif->sjf/dot_general | solution.py:12
  181.6 0.0 copy-start.4
  181.6 24.6 %copy.14 = f32[184,128,256]{1,0,2:T(8,128)} copy(f32[184,128,256]{2,1,0:T(8,128)} %fusion.4) | data formatting | bytes 48234496 | tf_op jit(solution)/shard_map/sij,sif->sjf/dot_general | solution.py:12
  206.2 0.0 copy-done.4
  206.2 0.0 copy-start.2
  206.2 0.0 copy-start.1
  206.2 17.1 %fusion.11 = bf16[32,256,128]{2,0,1:T(8,128)(2,1)S(1)} fusion(f32[184,128,256]{1,0,2:T(8,128)} %copy.14, s32[184]{0:T(256)S(1)} %bitcast.63, pred[184]{0:T(512)(128)(4,1)S(1)} %iota_compare_fusion.2), kind=kOutput, calls=%fused_computation.11 | convolution fusion | flops 2316322048 | bytes 26215320 | tf_op jit(solution)/shard_map/rs,sif->rif/dot_general | solution.py:28
  223.3 2.2 copy.12
  225.5 0.0 reduce-scatter.5.cloned.1.call-update
  225.5 0.0 all-gather.10.cloned.1.call-start
  225.5 0.0 reduce-scatter.3.cloned.1.call-done
  225.6 1.9 fusion.18
  227.4 0.0 all-gather.10.cloned.1.call-update
  227.4 0.0 copy-done.2
  227.4 1.9 fusion.14
  229.3 70.3 %reduce-scatter.5.cloned.1.call-done = bf16[1024,128]{1,0:T(8,128)(2,1)} async-done(((bf16[8192,128]{1,0:T(8,128)(2,1)}), bf16[1024,128]{1,0:T(8,128)(2,1)}) %reduce-scatter.5.cloned.1.call-update) | async-done | bytes 262160 | tf_op jit(solution)/shard_map/reduce_scatter | solution.py:70
  299.6 0.0 copy-done.1
  299.7 1.7 fusion.16
  301.4 203.3 %all-gather.10.cloned.1.call-done = f32[16384,128]{1,0:T(8,128)} async-done(((f32[128,128]{1,0:T(8,128)}), f32[16384,128]{1,0:T(8,128)}) %all-gather.10.cloned.1.call-update) | async-done | bytes 8388624 | tf_op jit(solution)/shard_map/all_gather | solution.py:63
  504.7 3.8 reduce_sum.9
  508.5 0.6 broadcast_multiply_fusion
  (4 shorter events, 0.0 us)
Async XLA Ops:
  7.2 2.0 copy-start
  7.2 60.7 %all-gather.8.cloned.1.call-start = ((), (), s32[]{:S(2)}) async-start(), calls=%async_computation.5 | async-start | bytes 2359296 | tf_op jit(solution)/shard_map/all_gather | solution.py:49
  9.1 140.1 %all-gather.6.cloned.1.call-start = ((), (), s32[]{:S(2)}) async-start(), calls=%async_computation.3 | async-start | bytes 4456448 | tf_op jit(solution)/shard_map/all_gather | solution.py:67
  10.9 214.6 %reduce-scatter.3.cloned.1.call-start = ((), (), s32[]{:S(2)}) async-start(), calls=%async_computation.2 | async-start | bytes 4456448 | tf_op jit(solution)/shard_map/reduce_scatter | solution.py:54
  99.1 24.6 %copy-start.3 = (s32[1,1,184]{2,1,0:T(1,128)S(1)}, s32[1,1,184]{2,1,0:T(1,128)}, u32[]{:S(2)}) copy-start(s32[1,1,184]{2,1,0:T(1,128)} %param.11) | copy-start | bytes 2212
  149.2 150.5 %reduce-scatter.5.cloned.1.call-start = ((), (), s32[]{:S(2)}) async-start(), calls=%async_computation.4 | async-start | bytes 2359296 | tf_op jit(solution)/shard_map/reduce_scatter | solution.py:70
  181.6 24.6 %copy-start.4 = (s32[1,1,184]{2,1,0:T(1,128)S(1)}, s32[1,1,184]{2,1,0:T(1,128)}, u32[]{:S(2)}) copy-start(s32[1,1,184]{2,1,0:T(1,128)} %param.12) | copy-start | bytes 2212
  206.2 21.2 %copy-start.2 = (bf16[128,128]{1,0:T(8,128)(2,1)S(1)}, bf16[128,128]{1,0:T(8,128)(2,1)}, u32[]{:S(2)}) copy-start(bf16[128,128]{1,0:T(8,128)(2,1)} %param.14) | copy-start | bytes 98308
  206.2 93.5 %copy-start.1 = (s32[1,1024,128]{2,1,0:T(8,128)S(1)}, s32[1,1024,128]{2,1,0:T(8,128)}, u32[]{:S(2)}) copy-start(s32[1,1024,128]{2,1,0:T(8,128)} %param.9) | copy-start | bytes 1572868
  225.5 279.2 %all-gather.10.cloned.1.call-start = ((), (), s32[]{:S(2)}) async-start(), calls=%async_computation.6 | async-start | bytes 8454144 | tf_op jit(solution)/shard_map/all_gather | solution.py:63
Sparse Core Ops, SparseCore 0:
  10.9 56.9 all-gather.7
  70.1 37.8 all-gather.5
  149.3 63.9 reduce-scatter.2
  225.6 74.0 reduce-scatter.4
  301.9 202.7 all-gather.9
